TPU v7x, 32 devices: a whole 2x2x4 slice. The times are simulated.
32 devices in a mesh: group: 2 (over x), dom: 16 (over z, y, core).
Axes of the slice: x: 2, y: 2, z: 4, core: 2. Of those that a mesh axis runs over, the one named last changes fastest.
Arguments:
- features: bfloat16 [8192, 512], P(('group', 'dom')), may hold values from -6 to 6
- tile_columns: int32 [32, 2, 4], P(('group', 'dom')), may hold values from 0 to 1
- tile_values: bfloat16 [32, 2, 4, 128, 128], P(('group', 'dom')), as said below
- send_rows: int32 [32, 16, 16], P(('group', 'dom')), may hold values from 0 to 255
- send_count: int32 [32, 16], P(('group', 'dom')), may hold values from 0 to 16, as said below
- ghost_target: int32 [32, 16, 16], P(('group', 'dom')), may hold values from 0 to 255
- query_rows: int32 [32, 512], P(('group', 'dom')), may hold values from 0 to 255
- positive_cand: int32 [32, 512], P(('group', 'dom')), may hold values from 0 to 63
- negative_rows: int32 [32, 32], P(('group', 'dom')), may hold values from 0 to 255
- weight_self: bfloat16 [512, 512], replicated, may hold values from -0.25 to 0.25
- weight_neigh: bfloat16 [512, 512], replicated, may hold values from -0.75 to 0.75
Outputs:
- embeddings: bfloat16 [8192, 512], P(('group', 'dom'))
- weight_grads: bfloat16 [1024, 512], P('dom')
Inputs may be any that keep to these rules, and one draw needn't show every extreme that they name: `send_count`: no device sends rows to its own index of dom; in every group one index of dom receives exactly 16 rows from every other index. `tile_values`: weights are zero or between 0.5 and 1.
All inputs are finite; a program needn't handle non-finite values.
Results may differ from a plain program's by a relative error of at most 0.015.
Values may be sent and summed in bfloat16 or wider, within the bound.
No kernel may reach another device: no remote copies, remote signals or barrier semaphores. Data moves between devices by JAX's collectives and lax.ppermute only.
A program may use at most 64 MiB of HBM per device.

v0:
```python
import math
import jax
import jax.numpy as jnp
from jax import lax
from jax.sharding import PartitionSpec as P

LOSS_FACTOR = 64.0
EPSILON = 1e-05


def score_grads(scores, positive, cand_total, query_total):
    sigma = jax.nn.sigmoid(scores)
    dscore = jnp.where(positive, sigma - 1.0, sigma / (cand_total - 1.0)) * (
        LOSS_FACTOR / query_total
    )
    return dscore.astype(jnp.bfloat16)


def transpose_dot(left, right):
    return lax.dot_general(
        left, right, (((0,), (0,)), ((), ())), preferred_element_type=jnp.float32
    )


def on_device(
    features,
    tile_columns,
    tile_values,
    send_rows,
    send_count,
    ghost_target,
    query_rows,
    positive_cand,
    negative_rows,
    weight_self,
    weight_neigh,
):
    node_count, width = features.shape
    row_blocks, tiles_row, tile_size = (
        tile_values.shape[1],
        tile_values.shape[2],
        tile_values.shape[3],
    )
    slot_count = send_rows.shape[2]
    group_count = lax.axis_size("group")
    score_factor = 1.0 / math.sqrt(width)
    outgoing = features[send_rows[0]]
    flags = (jnp.arange(slot_count, dtype=jnp.int32)[None, :] < send_count[0][:, None]).astype(
        jnp.bfloat16
    )
    received, flags_in = (
        lax.all_to_all(outgoing, "dom", split_axis=0, concat_axis=0, tiled=True),
        lax.all_to_all(flags, "dom", split_axis=0, concat_axis=0, tiled=True),
    )
    blocks = features.reshape(row_blocks, tile_size, width)
    picked = blocks[tile_columns[0]]
    local = jnp.einsum(
        "rtij,rtjd->rid", tile_values[0], picked, preferred_element_type=jnp.float32
    ).reshape(node_count, width)
    row_weight = jnp.sum(tile_values[0].astype(jnp.float32), axis=(1, 3)).reshape(node_count)
    live = flags_in.astype(jnp.float32)
    targets = ghost_target[0].reshape(-1)
    weighted = (received.astype(jnp.float32) * live[:, :, None]).reshape(-1, width)
    ghost_sum = jnp.zeros((node_count, width), jnp.float32).at[targets].add(weighted)
    ghost_count = jnp.zeros((node_count,), jnp.float32).at[targets].add(live.reshape(-1))
    degree = 1.0 + row_weight + ghost_count
    aggregate = ((local + ghost_sum) / degree[:, None]).astype(jnp.bfloat16)
    pre = jnp.dot(features, weight_self, preferred_element_type=jnp.float32) + jnp.dot(
        aggregate, weight_neigh, preferred_element_type=jnp.float32
    )
    scale = lax.rsqrt(jnp.mean(pre * pre, axis=-1, keepdims=True) + EPSILON)
    embeds = (pre * scale).astype(jnp.bfloat16)
    queries = embeds[query_rows[0]]
    own_negs = embeds[negative_rows[0]]
    neg_count = own_negs.shape[0]
    query_total = queries.shape[0]
    cand_total = neg_count * group_count
    targets_pos = positive_cand[0][:, None]
    all_negs = lax.all_gather(own_negs, "group", axis=0, tiled=True)
    scores = score_factor * jnp.dot(queries, all_negs.T, preferred_element_type=jnp.float32)
    positive = targets_pos == jnp.arange(cand_total, dtype=jnp.int32)[None, :]
    dscore = score_grads(scores, positive, cand_total, query_total)
    query_grad = score_factor * jnp.dot(dscore, all_negs, preferred_element_type=jnp.float32)
    neg_grad = lax.psum_scatter(
        (score_factor * transpose_dot(dscore, queries)).astype(jnp.bfloat16),
        "group",
        scatter_dimension=0,
        tiled=True,
    ).astype(jnp.float32)
    emb_grad = jnp.zeros((node_count, width), jnp.float32)
    emb_grad = emb_grad.at[query_rows[0]].add(query_grad)
    emb_grad = emb_grad.at[negative_rows[0]].add(neg_grad)
    inner = jnp.mean(pre * emb_grad, axis=-1, keepdims=True)
    pre_grad = (scale * emb_grad - pre * scale * scale * scale * inner).astype(jnp.bfloat16)
    stacked = jnp.concatenate([features, aggregate], axis=1)
    shard = lax.psum_scatter(
        transpose_dot(stacked, pre_grad), "dom", scatter_dimension=0, tiled=True
    )
    summed = lax.psum(shard.astype(jnp.bfloat16), "group")
    return (embeds, summed)


def solution(mesh):
    placed = (
        P(("group", "dom"), None),
        P(("group", "dom"), None, None),
        P(("group", "dom"), None, None, None, None),
        P(("group", "dom"), None, None),
        P(("group", "dom"), None),
        P(("group", "dom"), None, None),
        P(("group", "dom"), None),
        P(("group", "dom"), None),
        P(("group", "dom"), None),
        P(),
        P(),
    )
    return jax.shard_map(
        on_device,
        mesh=mesh,
        in_specs=placed,
        out_specs=(P(("group", "dom"), None), P("dom", None)),
        check_vma=False,
    )
```

profile of v0, /device:TPU:0, one launch (start us, length us, event | category | flops | bytes accessed | tf_op | source)
XLA Modules:
  0.0 157.0 jit_solution(12821754926774188139)
XLA Ops:
  7.2 0.0 copy-start
  7.2 0.0 copy-start.2
  7.2 1.4 compare_convert_fusion
  8.6 7.4 %all-to-all-start.1 = ((bf16[16,1,16]{2,1,0:T(2,128)(2,1)}), bf16[16,1,16]{2,1,0:T(2,128)(2,1)S(1)}, u32[]{:S(2)}, u32[]{:S(2)}) async-start(bf16[16,1,16]{2,1,0:T(2,128)(2,1)} %compare_convert_fusion), calls=%async_computation.1 | async-start | bytes 16384 | tf_op jit(solution)/shard_map/all_to_all | solution.py:53
  16.0 0.7 fusion.17
  16.7 0.7 compare_select_fusion.3
  17.4 0.1 reshape.231
  17.4 0.8 reshape_squeeze.3
  18.2 1.1 convert_reduce_fusion
  19.3 0.7 compare_select_fusion.1
  20.0 0.7 compare_select_fusion
  20.7 0.1 reshape.239
  20.8 1.4 fusion.19
  22.2 0.0 copy-done.2
  22.3 0.0 copy-start.3
  22.3 1.9 %gather_fusion.1 = bf16[256,512]{1,0:T(8,128)(2,1)} fusion(bf16[256,512]{1,0:T(8,128)(2,1)S(1)} %copy-done.2, s32[1024]{0:T(1024)S(1)} %pad_clamp_fusion.2), kind=kCustom, calls=%fused_computation.1 | custom fusion | bytes 525312 | tf_op jit(solution)/shard_map/gather | solution.py:47
  24.1 0.6 gather_fusion
  24.7 0.0 all-to-all-done.1
  24.8 6.0 %all-to-all-start = ((bf16[16,16,512]{2,1,0:T(8,128)(2,1)}), bf16[16,16,512]{2,1,0:T(8,128)(2,1)S(1)}, u32[]{:S(2)}, u32[]{:S(2)}) async-start(bf16[16,16,512]{2,1,0:T(8,128)(2,1)} %bitcast.10), calls=%async_computation | async-start | bytes 524288 | tf_op jit(solution)/shard_map/all_to_all | solution.py:52
  30.8 0.0 reduce-scatter.3.cloned.1.call-start
  30.8 0.0 copy-done.3
  30.9 0.3 fusion.9
  31.2 0.1 reshape.273
  31.3 2.3 %scatter_fusion.1 = f32[256]{0:T(256)S(1)} fusion(f32[256]{0:T(256)S(1)} %add_bitcast_fusion, s32[256]{0:T(256)S(1)} %bitcast.51, f32[256]{0:T(256)S(1)} %reshape.273), kind=kCustom, calls=%fused_computation.5 | custom fusion | flops 256 | bytes 4096 | tf_op jit(solution)/shard_map/scatter-add | solution.py:65
  33.6 7.2 %all-to-all-done = bf16[16,16,512]{2,1,0:T(8,128)(2,1)S(1)} async-done(((bf16[16,16,512]{2,1,0:T(8,128)(2,1)}), bf16[16,16,512]{2,1,0:T(8,128)(2,1)S(1)}, u32[]{:S(2)}, u32[]{:S(2)}) %all-to-all-start) | async-done | bytes 262176 | tf_op jit(solution)/shard_map/all_to_all | solution.py:52
  40.8 0.1 convert_multiply_fusion
  40.9 2.3 %scatter_fusion = f32[256,512]{1,0:T(8,128)S(1)} fusion(f32[256,512]{1,0:T(8,128)S(1)} %bitcast.46, s32[256]{0:T(256)S(1)} %bitcast.52, f32[256,512]{1,0:T(8,128)S(1)} %bitcast.49), kind=kCustom, calls=%fused_computation.4 | custom fusion | flops 131072 | bytes 1573888 | tf_op jit(solution)/shard_map/scatter-add | solution.py:64
  43.2 0.1 divide_convert_fusion
  43.3 0.0 copy-done
  43.3 0.4 multiply_reduce_fusion.1
  43.7 0.1 multiply_convert_fusion
  43.9 0.0 copy-start.1
  43.9 0.6 gather_fusion.3
  44.5 4.6 %all-gather = bf16[64,512]{1,0:T(8,128)(2,1)S(1)} all-gather(bf16[32,512]{1,0:T(8,128)(2,1)S(1)} %gather_fusion.3), channel_id=2, replica_groups=mesh['group'=2,'dom'=16] {'group'}, dimensions={0}, use_global_device_ids=true | all-gather | bytes 98304 | tf_op jit(solution)/shard_map/all_gather | solution.py:79
  49.1 0.0 copy-start.4
  49.1 2.0 %gather_fusion.2 = bf16[512,512]{1,0:T(8,128)(2,1)S(1)} fusion(bf16[256,512]{1,0:T(8,128)(2,1)S(1)} %multiply_convert_fusion, s32[1024]{0:T(1024)S(1)} %pad_clamp_fusion.1), kind=kCustom, calls=%fused_computation.2 | custom fusion | bytes 1050624 | tf_op jit(solution)/shard_map/gather | solution.py:73
  51.1 0.0 copy-done.1
  51.1 0.0 copy-done.4
  51.1 0.3 multiply_convert_fusion.1
  51.4 0.8 fusion.4
  52.3 0.0 reduce-scatter.3.cloned.1.call-update
  52.3 0.0 reduce-scatter.5.cloned.1.call-start
  52.3 0.3 convolution_multiply_fusion
  52.6 3.7 %scatter_custom_fusion.2 = f32[256,512]{1,0:T(8,128)S(1)} fusion(s32[512]{0:T(512)S(1)} %bitcast.54, f32[512,512]{1,0:T(8,128)S(1)} %convolution_multiply_fusion, f32[]{:T(128)} %constant.14.clone.1), kind=kCustom, calls=%fused_computation.31 | custom fusion | flops 262144 | bytes 524292 | tf_op jit(solution)/shard_map/scatter-add | solution.py:91
  56.4 4.3 %reduce-scatter.3.cloned.1.call-done = bf16[32,512]{1,0:T(8,128)(2,1)} async-done(((bf16[64,512]{1,0:T(8,128)(2,1)}), bf16[32,512]{1,0:T(8,128)(2,1)}) %reduce-scatter.3.cloned.1.call-update) | async-done | bytes 32784 | tf_op jit(solution)/shard_map/reduce_scatter | solution.py:84
  60.6 1.2 scatter_custom_fusion.3
  61.9 0.1 multiply_reduce_fusion
  62.0 2.0 %fusion.5 = f32[1024,512]{1,0:T(8,128)} fusion(bf16[256,512]{1,0:T(8,128)(2,1)S(1)} %divide_convert_fusion, bf16[256,512]{1,0:T(8,128)(2,1)S(1)} %copy-done.2, f32[256,512]{1,0:T(8,128)S(1)} %scatter_custom_fusion.3, f32[256,512]{1,0:T(8,128)S(1)} %get-tuple-element.3, f32[256]{0:T(256)S(1)} %broadcast_multiply_fusion, f32[256]{0:T(256)S(1)} %add_rsqrt_fusion), kind=kOutput, calls=%fused_computation.17 | convolution fusion | flops 270401536 | bytes 3672064 | tf_op jit(solution)/shard_map/dot_general | solution.py:20
  64.0 0.0 reduce-scatter.5.cloned.1.call-update
  64.0 0.0 all-reduce.2.cloned.1.call-start
  64.0 62.2 %reduce-scatter.5.cloned.1.call-done = f32[64,512]{1,0:T(8,128)} async-done(((f32[1024,512]{1,0:T(8,128)}), f32[64,512]{1,0:T(8,128)}) %reduce-scatter.5.cloned.1.call-update) | async-done | bytes 131088 | tf_op jit(solution)/shard_map/reduce_scatter | solution.py:96
  126.2 1.5 convert_element_type.66
  127.8 0.0 all-reduce.2.cloned.1.call-update
  127.8 21.2 %all-reduce.2.cloned.1.call-done = bf16[64,512]{1,0:T(8,128)(2,1)} async-done(((bf16[64,512]{1,0:T(8,128)(2,1)}), bf16[64,512]{1,0:T(8,128)(2,1)}) %all-reduce.2.cloned.1.call-update) | async-done | bytes 65552 | tf_op jit(solution)/shard_map/psum | solution.py:99
  149.0 1.5 copy.18
  (10 shorter events, 0.1 us)
Async XLA Ops:
  7.2 36.2 %copy-start = (bf16[512,512]{1,0:T(8,128)(2,1)S(1)}, bf16[512,512]{1,0:T(8,128)(2,1)}, u32[]{:S(2)}) copy-start(bf16[512,512]{1,0:T(8,128)(2,1)} %param.21) | copy-start | bytes 1572868
  7.2 15.1 %copy-start.2 = (bf16[256,512]{1,0:T(8,128)(2,1)S(1)}, bf16[256,512]{1,0:T(8,128)(2,1)}, u32[]{:S(2)}) copy-start(bf16[256,512]{1,0:T(8,128)(2,1)} %param.11) | copy-start | bytes 786436
  8.6 16.1 %all-to-all-start.1 = ((bf16[16,1,16]{2,1,0:T(2,128)(2,1)}), bf16[16,1,16]{2,1,0:T(2,128)(2,1)S(1)}, u32[]{:S(2)}, u32[]{:S(2)}) async-start(bf16[16,1,16]{2,1,0:T(2,128)(2,1)} %compare_convert_fusion), calls=%async_computation.1 | async-start | bytes 16384 | tf_op jit(solution)/shard_map/all_to_all | solution.py:53
  22.3 8.6 %copy-start.3 = (bf16[1,2,4,128,128]{4,3,2,1,0:T(8,128)(2,1)S(1)}, bf16[1,2,4,128,128]{4,3,2,1,0:T(8,128)(2,1)}, u32[]{:S(2)}) copy-start(bf16[1,2,4,128,128]{4,3,2,1,0:T(8,128)(2,1)} %param.13) | copy-start | bytes 786436
  24.8 16.0 %all-to-all-start = ((bf16[16,16,512]{2,1,0:T(8,128)(2,1)}), bf16[16,16,512]{2,1,0:T(8,128)(2,1)S(1)}, u32[]{:S(2)}, u32[]{:S(2)}) async-start(bf16[16,16,512]{2,1,0:T(8,128)(2,1)} %bitcast.10), calls=%async_computation | async-start | bytes 524288 | tf_op jit(solution)/shard_map/all_to_all | solution.py:52
  30.8 29.9 %reduce-scatter.3.cloned.1.call-start = ((), (), s32[]{:S(2)}) async-start(), calls=%async_computation.4 | async-start | bytes 98304 | tf_op jit(solution)/shard_map/reduce_scatter | solution.py:84
  43.9 7.2 %copy-start.1 = (bf16[256,512]{1,0:T(8,128)(2,1)}, bf16[256,512]{1,0:T(8,128)(2,1)S(1)}, u32[]{:S(2)}) copy-start(bf16[256,512]{1,0:T(8,128)(2,1)S(1)} %multiply_convert_fusion) | copy-start | bytes 786436
  49.1 2.0 %copy-start.4 = (s32[1,512]{1,0:T(1,128)S(1)}, s32[1,512]{1,0:T(1,128)}, u32[]{:S(2)}) copy-start(s32[1,512]{1,0:T(1,128)} %param.18) | copy-start | bytes 6148
  52.3 74.0 %reduce-scatter.5.cloned.1.call-start = ((), (), s32[]{:S(2)}) async-start(), calls=%async_computation.5 | async-start | bytes 2228224 | tf_op jit(solution)/shard_map/reduce_scatter | solution.py:96
  64.0 85.0 %all-reduce.2.cloned.1.call-start = ((), (), s32[]{:S(2)}) async-start(), calls=%async_computation.6 | async-start | bytes 131072 | tf_op jit(solution)/shard_map/psum | solution.py:99
Sparse Core Ops, SparseCore 0:
  52.4 8.1 reduce-scatter.2
  64.4 61.8 reduce-scatter.4
  129.1 19.8 all-reduce.1
where the time goes:
time: 158 us; the launch traced here: 157 us
  waiting for transfers between devices  94.9 us (60%)
  other arithmetic  16.8 us (11%)
  between operations  14 us (9%)
  starting transfers between devices  13.6 us (9%)
  local copies, waits for them, and re-layouts  7.58 us (5%)
  matrix products  5.54 us (4%)
  blocking collectives  4.58 us (3%)
    reduce_scatter x1, waiting for transfers between devices, on_device(): lax.psum_scatter(transpose_dot(stacked, pre_grad), 'dom', scatter_dimensi...  62.2 us
    psum x1, waiting for transfers between devices, on_device(): summed = lax.psum(shard.astype(jnp.bfloat16), 'group')  21.2 us
    all_to_all x1, starting transfers between devices, on_device(): lax.all_to_all(flags, 'dom', split_axis=0, concat_axis=0, tiled=True)  7.41 us
    all_to_all x1, waiting for transfers between devices, on_device(): lax.all_to_all(outgoing, 'dom', split_axis=0, concat_axis=0, tiled=True)  7.18 us
    all_to_all x1, starting transfers between devices, on_device(): lax.all_to_all(outgoing, 'dom', split_axis=0, concat_axis=0, tiled=True)  6.02 us
    all_gather x1, blocking collectives, on_device(): all_negs = lax.all_gather(own_negs, 'group', axis=0, tiled=True)  4.58 us
    reduce_scatter x1, waiting for transfers between devices, on_device(): lax.psum_scatter((score_factor * transpose_dot(dscore, queries)).astype(j...  4.28 us
    scatter-add x1, other arithmetic, on_device(): emb_grad = emb_grad.at[query_rows[0]].add(query_grad)  3.71 us
  transfers between devices with their start and end apart: 5, of which 4 were waited for; matrix products, arithmetic and copies ran while one was open for 10% of the time, Pallas kernels for 0%

commit v1 on v0

--- a/solution.py
+++ b/solution.py
@@ -6,6 +6,30 @@
 
 LOSS_FACTOR = 64.0
 EPSILON = 1e-05
+
+
+def cut_along(x, dim, count):
+    shape = x.shape
+    parts = x.reshape(*shape[:dim], count, shape[dim] // count, *shape[dim + 1 :])
+    return jnp.moveaxis(parts, dim, 0)
+
+
+def in_order(tiles, dim):
+    tiles = jnp.moveaxis(tiles, 0, dim)
+    lengths = tiles.shape
+    return tiles.reshape(*lengths[:dim], lengths[dim] * lengths[dim + 1], *lengths[dim + 2 :])
+
+
+def rotated_exchange(value, axis, split_dim, concat_dim):
+    size, index = (lax.axis_size(axis), lax.axis_index(axis))
+    pieces = cut_along(value, split_dim, size)
+    out = pieces
+    for step in range(1, size):
+        target, source = ((index + step) % size, (index - step) % size)
+        sent = lax.dynamic_index_in_dim(pieces, target, 0)
+        other = lax.ppermute(sent, axis, [(i, (i + step) % size) for i in range(size)])
+        out = lax.dynamic_update_slice_in_dim(out, other, source, axis=0)
+    return in_order(out, concat_dim)
 
 
 def score_grads(scores, positive, cand_total, query_total):
@@ -49,7 +73,7 @@
         jnp.bfloat16
     )
     received, flags_in = (
-        lax.all_to_all(outgoing, "dom", split_axis=0, concat_axis=0, tiled=True),
+        rotated_exchange(outgoing, "dom", 0, 0),
         lax.all_to_all(flags, "dom", split_axis=0, concat_axis=0, tiled=True),
     )
     blocks = features.reshape(row_blocks, tile_size, width)

time: 158 us -> 196 us (1.24)
  waiting for transfers between devices: 94.9 us -> 130 us
  starting transfers between devices: 13.6 us -> 20.3 us
  other arithmetic: 16.8 us -> 13.9 us
    ppermute x0 -> x15, waiting for transfers between devices: none -> 38.3 us  [rotated_exchange(): lax.ppermute(sent, axis, [(i, (i + step) % size) for i in range(size)])]
    ppermute x0 -> x15, starting transfers between devices: none -> 12.7 us  [rotated_exchange(): lax.ppermute(sent, axis, [(i, (i + step) % size) for i in range(size)])]
    all_to_all x1 -> x0, waiting for transfers between devices: 7.18 us -> none  [on_device(): lax.all_to_all(outgoing, 'dom', split_axis=0, concat_axis=0, tiled=True)]
    all_to_all x1 -> x0, starting transfers between devices: 6.02 us -> none  [on_device(): lax.all_to_all(outgoing, 'dom', split_axis=0, concat_axis=0, tiled=True)]
    reduce_scatter x1, waiting for transfers between devices: 4.28 us -> 8.53 us  [on_device(): lax.psum_scatter((score_factor * transpose_dot(dscore, queries)).astype(j...]
  transfers between devices with their start and end apart: 5 -> 19, of which waited for: 4 -> 13; matrix products, arithmetic and copies ran while one was open for 10% -> 6% of each run, Pallas kernels for 0% -> 0%
where the time goes in v1:
time: 196 us; the launch traced here: 195 us
  waiting for transfers between devices  130 us (66%)
  starting transfers between devices  20.3 us (10%)
  between operations  14.6 us (7%)
  other arithmetic  13.9 us (7%)
  local copies, waits for them, and re-layouts  7.33 us (4%)
  blocking collectives  4.58 us (2%)
  matrix products  4.43 us (2%)
    reduce_scatter x1, waiting for transfers between devices, on_device(): lax.psum_scatter(transpose_dot(stacked, pre_grad), 'dom', scatter_dimensi...  62.2 us
    ppermute x15, waiting for transfers between devices, rotated_exchange(): lax.ppermute(sent, axis, [(i, (i + step) % size) for i in range(size)])  38.3 us
    psum x1, waiting for transfers between devices, on_device(): summed = lax.psum(shard.astype(jnp.bfloat16), 'group')  21.2 us
    ppermute x15, starting transfers between devices, rotated_exchange(): lax.ppermute(sent, axis, [(i, (i + step) % size) for i in range(size)])  12.7 us
    reduce_scatter x1, waiting for transfers between devices, on_device(): lax.psum_scatter((score_factor * transpose_dot(dscore, queries)).astype(j...  8.53 us
    all_to_all x1, starting transfers between devices, on_device(): lax.all_to_all(flags, 'dom', split_axis=0, concat_axis=0, tiled=True)  7.41 us
    all_gather x1, blocking collectives, on_device(): all_negs = lax.all_gather(own_negs, 'group', axis=0, tiled=True)  4.58 us
  transfers between devices with their start and end apart: 19, of which 13 were waited for; matrix products, arithmetic and copies ran while one was open for 6% of the time, Pallas kernels for 0%

profile of v1, /device:TPU:0, one launch (start us, length us, event | category | flops | bytes accessed | tf_op | source)
XLA Modules:
  0.0 195.4 jit_solution(13757445732330636953)
XLA Ops:
  7.2 0.0 copy-start
  7.2 0.0 copy-start.2
  7.3 1.4 compare_convert_fusion
  8.7 7.4 %all-to-all-start = ((bf16[16,1,16]{2,1,0:T(2,128)(2,1)}), bf16[16,1,16]{2,1,0:T(2,128)(2,1)S(1)}, u32[]{:S(2)}, u32[]{:S(2)}) async-start(bf16[16,1,16]{2,1,0:T(2,128)(2,1)} %compare_convert_fusion), calls=%async_computation | async-start | bytes 16384 | tf_op jit(solution)/shard_map/all_to_all | solution.py:77
  16.1 0.0 reduce-scatter.3.cloned.1.call-start
  16.2 0.7 compare_select_fusion
  16.9 0.1 reshape.332
  17.0 2.2 %gather_fusion.1 = bf16[256,512]{1,0:T(8,128)(2,1)S(1)} fusion(bf16[256,512]{1,0:T(8,128)(2,1)} %param.11, s32[1024]{0:T(1024)S(1)} %pad_clamp_fusion.2), kind=kCustom, calls=%fused_computation.1 | custom fusion | bytes 525312 | tf_op jit(solution)/shard_map/gather | solution.py:71
  19.2 0.5 collective-permute-start
  19.7 0.1 reshape.324
  19.8 0.1 reshape_squeeze.3
  19.9 0.1 convert_reduce_fusion
  20.1 0.3 fusion.19
  20.4 0.6 gather_fusion
  21.0 0.3 fusion.9
  21.7 3.4 %collective-permute-done = bf16[1,1,16,512]{3,2,1,0:T(8,128)(2,1)S(1)} collective-permute-done((bf16[1,1,16,512]{3,2,1,0:T(8,128)(2,1)S(1)}, bf16[1,1,16,512]{3,2,1,0:T(8,128)(2,1)S(1)}, u32[]{:S(2)}, u32[]{:S(2)}) %collective-permute-start) | collective-permute-done | bytes 16416 | tf_op jit(solution)/shard_map/ppermute | solution.py:30
  25.1 0.1 collective-permute-start.1
  25.2 0.1 reshape.366
  25.3 2.3 %scatter_fusion.1 = f32[256]{0:T(256)S(1)} fusion(f32[256]{0:T(256)S(1)} %add_bitcast_fusion, s32[256]{0:T(256)S(1)} %bitcast.113, f32[256]{0:T(256)S(1)} %reshape.366), kind=kCustom, calls=%fused_computation.5 | custom fusion | flops 256 | bytes 4096 | tf_op jit(solution)/shard_map/scatter-add | solution.py:89
  27.7 2.4 %collective-permute-start.14 = (bf16[1,1,16,512]{3,2,1,0:T(8,128)(2,1)S(1)}, bf16[1,1,16,512]{3,2,1,0:T(8,128)(2,1)S(1)}, u32[]{:S(2)}, u32[]{:S(2)}) collective-permute-start(bf16[1,1,16,512]{3,2,1,0:T(8,128)(2,1)S(1)} %get-tuple-element.2), channel_id=1, source_target_pairs={{0,15},{1,0},{2,1},{3,2},{4,3},{5,4},{6,5},{7,6},{8,7},{9,8},{10,9... | collective-permute-start | bytes 49160 | tf_op jit(solution)/shard_map/ppermute | solution.py:30
  30.1 2.4 %collective-permute-start.13 = (bf16[1,1,16,512]{3,2,1,0:T(8,128)(2,1)S(1)}, bf16[1,1,16,512]{3,2,1,0:T(8,128)(2,1)S(1)}, u32[]{:S(2)}, u32[]{:S(2)}) collective-permute-start(bf16[1,1,16,512]{3,2,1,0:T(8,128)(2,1)S(1)} %get-tuple-element.3), channel_id=1, source_target_pairs={{0,14},{1,15},{2,0},{3,1},{4,2},{5,3},{6,4},{7,5},{8,6},{9,7},{10,... | collective-permute-start | bytes 49160 | tf_op jit(solution)/shard_map/ppermute | solution.py:30
  32.5 0.0 collective-permute-start.12
  32.5 0.5 collective-permute-start.11
  32.9 0.0 collective-permute-done.1
  32.9 1.3 collective-permute-start.2
  34.2 3.7 %collective-permute-done.2 = bf16[1,1,16,512]{3,2,1,0:T(8,128)(2,1)S(1)} collective-permute-done((bf16[1,1,16,512]{3,2,1,0:T(8,128)(2,1)S(1)}, bf16[1,1,16,512]{3,2,1,0:T(8,128)(2,1)S(1)}, u32[]{:S(2)}, u32[]{:S(2)}) %collective-permute-start.2) | collective-permute-done | bytes 16416 | tf_op jit(solution)/shard_map/ppermute | solution.py:30
  37.9 5.5 %collective-permute-done.3 = bf16[1,1,16,512]{3,2,1,0:T(8,128)(2,1)S(1)} collective-permute-done((bf16[1,1,16,512]{3,2,1,0:T(8,128)(2,1)S(1)}, bf16[1,1,16,512]{3,2,1,0:T(8,128)(2,1)S(1)}, u32[]{:S(2)}, u32[]{:S(2)}) %collective-permute-start.3) | collective-permute-done | bytes 16416 | tf_op jit(solution)/shard_map/ppermute | solution.py:30
  43.5 5.0 %collective-permute-done.4 = bf16[1,1,16,512]{3,2,1,0:T(8,128)(2,1)S(1)} collective-permute-done((bf16[1,1,16,512]{3,2,1,0:T(8,128)(2,1)S(1)}, bf16[1,1,16,512]{3,2,1,0:T(8,128)(2,1)S(1)}, u32[]{:S(2)}, u32[]{:S(2)}) %collective-permute-start.4) | collective-permute-done | bytes 16416 | tf_op jit(solution)/shard_map/ppermute | solution.py:30
  48.4 5.5 %collective-permute-done.5 = bf16[1,1,16,512]{3,2,1,0:T(8,128)(2,1)S(1)} collective-permute-done((bf16[1,1,16,512]{3,2,1,0:T(8,128)(2,1)S(1)}, bf16[1,1,16,512]{3,2,1,0:T(8,128)(2,1)S(1)}, u32[]{:S(2)}, u32[]{:S(2)}) %collective-permute-start.5) | collective-permute-done | bytes 16416 | tf_op jit(solution)/shard_map/ppermute | solution.py:30
  54.0 4.1 %collective-permute-done.6 = bf16[1,1,16,512]{3,2,1,0:T(8,128)(2,1)S(1)} collective-permute-done((bf16[1,1,16,512]{3,2,1,0:T(8,128)(2,1)S(1)}, bf16[1,1,16,512]{3,2,1,0:T(8,128)(2,1)S(1)}, u32[]{:S(2)}, u32[]{:S(2)}) %collective-permute-start.6) | collective-permute-done | bytes 16416 | tf_op jit(solution)/shard_map/ppermute | solution.py:30
  58.0 0.1 collective-permute-start.7
  58.1 4.6 %collective-permute-done.7 = bf16[1,1,16,512]{3,2,1,0:T(8,128)(2,1)S(1)} collective-permute-done((bf16[1,1,16,512]{3,2,1,0:T(8,128)(2,1)S(1)}, bf16[1,1,16,512]{3,2,1,0:T(8,128)(2,1)S(1)}, u32[]{:S(2)}, u32[]{:S(2)}) %collective-permute-start.7) | collective-permute-done | bytes 16416 | tf_op jit(solution)/shard_map/ppermute | solution.py:30
  62.6 0.7 collective-permute-start.8
  63.4 3.3 %collective-permute-done.8 = bf16[1,1,16,512]{3,2,1,0:T(8,128)(2,1)S(1)} collective-permute-done((bf16[1,1,16,512]{3,2,1,0:T(8,128)(2,1)S(1)}, bf16[1,1,16,512]{3,2,1,0:T(8,128)(2,1)S(1)}, u32[]{:S(2)}, u32[]{:S(2)}) %collective-permute-start.8) | collective-permute-done | bytes 16416 | tf_op jit(solution)/shard_map/ppermute | solution.py:30
  66.7 2.8 %collective-permute-start.9 = (bf16[1,1,16,512]{3,2,1,0:T(8,128)(2,1)S(1)}, bf16[1,1,16,512]{3,2,1,0:T(8,128)(2,1)S(1)}, u32[]{:S(2)}, u32[]{:S(2)}) collective-permute-start(bf16[1,1,16,512]{3,2,1,0:T(8,128)(2,1)S(1)} %get-tuple-element.7), channel_id=1, source_target_pairs={{0,10},{1,11},{2,12},{3,13},{4,14},{5,15},{6,0},{7,1},{8,2},{9,3},... | collective-permute-start | bytes 49160 | tf_op jit(solution)/shard_map/ppermute | solution.py:30
  69.5 1.9 collective-permute-done.9
  71.3 2.1 %collective-permute-start.10 = (bf16[1,1,16,512]{3,2,1,0:T(8,128)(2,1)S(1)}, bf16[1,1,16,512]{3,2,1,0:T(8,128)(2,1)S(1)}, u32[]{:S(2)}, u32[]{:S(2)}) collective-permute-start(bf16[1,1,16,512]{3,2,1,0:T(8,128)(2,1)S(1)} %get-tuple-element.6), channel_id=1, source_target_pairs={{0,11},{1,12},{2,13},{3,14},{4,15},{5,0},{6,1},{7,2},{8,3},{9,4},{... | collective-permute-start | bytes 49160 | tf_op jit(solution)/shard_map/ppermute | solution.py:30
  73.4 1.4 collective-permute-done.10
  74.9 0.1 convert_multiply_fusion
  75.1 2.3 %scatter_fusion = f32[256,512]{1,0:T(8,128)S(1)} fusion(f32[256,512]{1,0:T(8,128)S(1)} %bitcast.106, s32[256]{0:T(256)S(1)} %bitcast.114, f32[256,512]{1,0:T(8,128)S(1)} %bitcast.111), kind=kCustom, calls=%fused_computation.4 | custom fusion | flops 131072 | bytes 1573888 | tf_op jit(solution)/shard_map/scatter-add | solution.py:88
  77.4 0.1 divide_convert_fusion
  77.5 0.4 multiply_reduce_fusion.1
  77.9 0.1 multiply_convert_fusion
  78.0 0.0 copy-start.1
  78.0 0.6 gather_fusion.3
  78.7 4.6 %all-gather = bf16[64,512]{1,0:T(8,128)(2,1)S(1)} all-gather(bf16[32,512]{1,0:T(8,128)(2,1)S(1)} %gather_fusion.3), channel_id=2, replica_groups=mesh['group'=2,'dom'=16] {'group'}, dimensions={0}, use_global_device_ids=true | all-gather | bytes 98304 | tf_op jit(solution)/shard_map/all_gather | solution.py:103
  83.2 2.0 %gather_fusion.2 = bf16[512,512]{1,0:T(8,128)(2,1)S(1)} fusion(bf16[256,512]{1,0:T(8,128)(2,1)S(1)} %multiply_convert_fusion, s32[1024]{0:T(1024)S(1)} %pad_clamp_fusion.1), kind=kCustom, calls=%fused_computation.2 | custom fusion | bytes 1050624 | tf_op jit(solution)/shard_map/gather | solution.py:97
  85.2 0.3 multiply_convert_fusion.1
  85.6 0.8 fusion.4
  86.4 0.0 reduce-scatter.3.cloned.1.call-update
  86.4 0.0 reduce-scatter.5.cloned.1.call-start
  86.5 0.3 convolution_multiply_fusion
  86.8 3.7 %scatter_custom_fusion.2 = f32[256,512]{1,0:T(8,128)S(1)} fusion(s32[512]{0:T(512)S(1)} %bitcast.116, f32[512,512]{1,0:T(8,128)S(1)} %convolution_multiply_fusion, f32[]{:T(128)} %constant.267.clone.1), kind=kCustom, calls=%fused_computation.31 | custom fusion | flops 262144 | bytes 524292 | tf_op jit(solution)/shard_map/scatter-add | solution.py:115
  90.5 8.5 %reduce-scatter.3.cloned.1.call-done = bf16[32,512]{1,0:T(8,128)(2,1)} async-done(((bf16[64,512]{1,0:T(8,128)(2,1)}), bf16[32,512]{1,0:T(8,128)(2,1)}) %reduce-scatter.3.cloned.1.call-update) | async-done | bytes 32784 | tf_op jit(solution)/shard_map/reduce_scatter | solution.py:108
  99.1 1.2 scatter_custom_fusion.3
  100.3 0.1 multiply_reduce_fusion
  100.4 2.0 fusion.5
  102.4 0.0 reduce-scatter.5.cloned.1.call-update
  102.4 0.0 all-reduce.2.cloned.1.call-start
  102.5 62.2 %reduce-scatter.5.cloned.1.call-done = f32[64,512]{1,0:T(8,128)} async-done(((f32[1024,512]{1,0:T(8,128)}), f32[64,512]{1,0:T(8,128)}) %reduce-scatter.5.cloned.1.call-update) | async-done | bytes 131088 | tf_op jit(solution)/shard_map/reduce_scatter | solution.py:120
  164.6 1.5 convert_element_type.66
  166.2 0.0 all-reduce.2.cloned.1.call-update
  166.2 21.2 %all-reduce.2.cloned.1.call-done = bf16[64,512]{1,0:T(8,128)(2,1)} async-done(((bf16[64,512]{1,0:T(8,128)(2,1)}), bf16[64,512]{1,0:T(8,128)(2,1)}) %all-reduce.2.cloned.1.call-update) | async-done | bytes 65552 | tf_op jit(solution)/shard_map/psum | solution.py:123
  187.4 1.5 copy.33
  (55 shorter events, 0.2 us)
Async XLA Ops:
  7.2 70.3 %copy-start = (bf16[512,512]{1,0:T(8,128)(2,1)S(1)}, bf16[512,512]{1,0:T(8,128)(2,1)}, u32[]{:S(2)}) copy-start(bf16[512,512]{1,0:T(8,128)(2,1)} %param.21) | copy-start | bytes 1572868
  7.2 12.9 %copy-start.2 = (bf16[256,512]{1,0:T(8,128)(2,1)S(1)}, bf16[256,512]{1,0:T(8,128)(2,1)}, u32[]{:S(2)}) copy-start(bf16[256,512]{1,0:T(8,128)(2,1)} %param.11) | copy-start | bytes 786436
  7.2 12.5 %copy-start.9 = (s32[1,32]{1,0:T(1,128)S(1)}, s32[1,32]{1,0:T(1,128)}, u32[]{:S(2)}) copy-start(s32[1,32]{1,0:T(1,128)} %param.19) | copy-start | bytes 388
  7.2 12.5 %copy-start.7 = (s32[1,2,4]{2,1,0:T(2,128)S(1)}, s32[1,2,4]{2,1,0:T(2,128)}, u32[]{:S(2)}) copy-start(s32[1,2,4]{2,1,0:T(2,128)} %param.12) | copy-start | bytes 100
  7.2 12.5 %copy-start.5 = (s32[1,16,16]{2,1,0:T(8,128)S(1)}, s32[1,16,16]{2,1,0:T(8,128)}, u32[]{:S(2)}) copy-start(s32[1,16,16]{2,1,0:T(8,128)} %param.16) | copy-start | bytes 3076
  7.2 12.6 %copy-start.3 = (bf16[1,2,4,128,128]{4,3,2,1,0:T(8,128)(2,1)S(1)}, bf16[1,2,4,128,128]{4,3,2,1,0:T(8,128)(2,1)}, u32[]{:S(2)}) copy-start(bf16[1,2,4,128,128]{4,3,2,1,0:T(8,128)(2,1)} %param.13) | copy-start | bytes 786436
  7.2 12.8 %copy-start.6 = (s32[1,512]{1,0:T(1,128)S(1)}, s32[1,512]{1,0:T(1,128)}, u32[]{:S(2)}) copy-start(s32[1,512]{1,0:T(1,128)} %param.17) | copy-start | bytes 6148
  7.2 12.8 %copy-start.4 = (bf16[512,512]{1,0:T(8,128)(2,1)S(1)}, bf16[512,512]{1,0:T(8,128)(2,1)}, u32[]{:S(2)}) copy-start(bf16[512,512]{1,0:T(8,128)(2,1)} %param.20) | copy-start | bytes 1572868
  8.7 16.5 %all-to-all-start = ((bf16[16,1,16]{2,1,0:T(2,128)(2,1)}), bf16[16,1,16]{2,1,0:T(2,128)(2,1)S(1)}, u32[]{:S(2)}, u32[]{:S(2)}) async-start(bf16[16,1,16]{2,1,0:T(2,128)(2,1)} %compare_convert_fusion), calls=%async_computation | async-start | bytes 16384 | tf_op jit(solution)/shard_map/all_to_all | solution.py:77
  16.1 82.9 %reduce-scatter.3.cloned.1.call-start = ((), (), s32[]{:S(2)}) async-start(), calls=%async_computation.3 | async-start | bytes 98304 | tf_op jit(solution)/shard_map/reduce_scatter | solution.py:108
  19.2 5.9 %collective-permute-start = (bf16[1,1,16,512]{3,2,1,0:T(8,128)(2,1)S(1)}, bf16[1,1,16,512]{3,2,1,0:T(8,128)(2,1)S(1)}, u32[]{:S(2)}, u32[]{:S(2)}) collective-permute-start(bf16[1,1,16,512]{3,2,1,0:T(8,128)(2,1)S(1)} %dynamic-slice_bitcast_fusion.14), channel_id=1, source_target_pairs={{0,1},{1,2},{2,3},{3,4},{4,5},{5,6},{6,7},{7,8},{8,9},{9,10},{10,1... | collective-permute-start | bytes 49160 | tf_op jit(solution)/shard_map/ppermute | solution.py:30
  25.1 7.8 %collective-permute-start.1 = (bf16[1,1,16,512]{3,2,1,0:T(8,128)(2,1)S(1)}, bf16[1,1,16,512]{3,2,1,0:T(8,128)(2,1)S(1)}, u32[]{:S(2)}, u32[]{:S(2)}) collective-permute-start(bf16[1,1,16,512]{3,2,1,0:T(8,128)(2,1)S(1)} %get-tuple-element.15), channel_id=1, source_target_pairs={{0,2},{1,3},{2,4},{3,5},{4,6},{5,7},{6,8},{7,9},{8,10},{9,11},{10,... | collective-permute-start | bytes 49160 | tf_op jit(solution)/shard_map/ppermute | solution.py:30
  27.7 47.3 %collective-permute-start.14 = (bf16[1,1,16,512]{3,2,1,0:T(8,128)(2,1)S(1)}, bf16[1,1,16,512]{3,2,1,0:T(8,128)(2,1)S(1)}, u32[]{:S(2)}, u32[]{:S(2)}) collective-permute-start(bf16[1,1,16,512]{3,2,1,0:T(8,128)(2,1)S(1)} %get-tuple-element.2), channel_id=1, source_target_pairs={{0,15},{1,0},{2,1},{3,2},{4,3},{5,4},{6,5},{7,6},{8,7},{9,8},{10,9... | collective-permute-start | bytes 49160 | tf_op jit(solution)/shard_map/ppermute | solution.py:30
  30.1 44.8 %collective-permute-start.13 = (bf16[1,1,16,512]{3,2,1,0:T(8,128)(2,1)S(1)}, bf16[1,1,16,512]{3,2,1,0:T(8,128)(2,1)S(1)}, u32[]{:S(2)}, u32[]{:S(2)}) collective-permute-start(bf16[1,1,16,512]{3,2,1,0:T(8,128)(2,1)S(1)} %get-tuple-element.3), channel_id=1, source_target_pairs={{0,14},{1,15},{2,0},{3,1},{4,2},{5,3},{6,4},{7,5},{8,6},{9,7},{10,... | collective-permute-start | bytes 49160 | tf_op jit(solution)/shard_map/ppermute | solution.py:30
  32.5 42.4 %collective-permute-start.12 = (bf16[1,1,16,512]{3,2,1,0:T(8,128)(2,1)S(1)}, bf16[1,1,16,512]{3,2,1,0:T(8,128)(2,1)S(1)}, u32[]{:S(2)}, u32[]{:S(2)}) collective-permute-start(bf16[1,1,16,512]{3,2,1,0:T(8,128)(2,1)S(1)} %get-tuple-element.4), channel_id=1, source_target_pairs={{0,13},{1,14},{2,15},{3,0},{4,1},{5,2},{6,3},{7,4},{8,5},{9,6},{10... | collective-permute-start | bytes 49160 | tf_op jit(solution)/shard_map/ppermute | solution.py:30
  32.5 42.4 %collective-permute-start.11 = (bf16[1,1,16,512]{3,2,1,0:T(8,128)(2,1)S(1)}, bf16[1,1,16,512]{3,2,1,0:T(8,128)(2,1)S(1)}, u32[]{:S(2)}, u32[]{:S(2)}) collective-permute-start(bf16[1,1,16,512]{3,2,1,0:T(8,128)(2,1)S(1)} %get-tuple-element.5), channel_id=1, source_target_pairs={{0,12},{1,13},{2,14},{3,15},{4,0},{5,1},{6,2},{7,3},{8,4},{9,5},{1... | collective-permute-start | bytes 49160 | tf_op jit(solution)/shard_map/ppermute | solution.py:30
  32.9 5.0 %collective-permute-start.2 = (bf16[1,1,16,512]{3,2,1,0:T(8,128)(2,1)S(1)}, bf16[1,1,16,512]{3,2,1,0:T(8,128)(2,1)S(1)}, u32[]{:S(2)}, u32[]{:S(2)}) collective-permute-start(bf16[1,1,16,512]{3,2,1,0:T(8,128)(2,1)S(1)} %get-tuple-element.14), channel_id=1, source_target_pairs={{0,3},{1,4},{2,5},{3,6},{4,7},{5,8},{6,9},{7,10},{8,11},{9,12},{10... | collective-permute-start | bytes 49160 | tf_op jit(solution)/shard_map/ppermute | solution.py:30
  37.9 5.5 %collective-permute-start.3 = (bf16[1,1,16,512]{3,2,1,0:T(8,128)(2,1)S(1)}, bf16[1,1,16,512]{3,2,1,0:T(8,128)(2,1)S(1)}, u32[]{:S(2)}, u32[]{:S(2)}) collective-permute-start(bf16[1,1,16,512]{3,2,1,0:T(8,128)(2,1)S(1)} %get-tuple-element.13), channel_id=1, source_target_pairs={{0,4},{1,5},{2,6},{3,7},{4,8},{5,9},{6,10},{7,11},{8,12},{9,13},{1... | collective-permute-start | bytes 49160 | tf_op jit(solution)/shard_map/ppermute | solution.py:30
  43.4 5.0 %collective-permute-start.4 = (bf16[1,1,16,512]{3,2,1,0:T(8,128)(2,1)S(1)}, bf16[1,1,16,512]{3,2,1,0:T(8,128)(2,1)S(1)}, u32[]{:S(2)}, u32[]{:S(2)}) collective-permute-start(bf16[1,1,16,512]{3,2,1,0:T(8,128)(2,1)S(1)} %get-tuple-element.12), channel_id=1, source_target_pairs={{0,5},{1,6},{2,7},{3,8},{4,9},{5,10},{6,11},{7,12},{8,13},{9,14},{... | collective-permute-start | bytes 49160 | tf_op jit(solution)/shard_map/ppermute | solution.py:30
  48.4 5.5 %collective-permute-start.5 = (bf16[1,1,16,512]{3,2,1,0:T(8,128)(2,1)S(1)}, bf16[1,1,16,512]{3,2,1,0:T(8,128)(2,1)S(1)}, u32[]{:S(2)}, u32[]{:S(2)}) collective-permute-start(bf16[1,1,16,512]{3,2,1,0:T(8,128)(2,1)S(1)} %get-tuple-element.11), channel_id=1, source_target_pairs={{0,6},{1,7},{2,8},{3,9},{4,10},{5,11},{6,12},{7,13},{8,14},{9,15},... | collective-permute-start | bytes 49160 | tf_op jit(solution)/shard_map/ppermute | solution.py:30
  53.9 4.1 %collective-permute-start.6 = (bf16[1,1,16,512]{3,2,1,0:T(8,128)(2,1)S(1)}, bf16[1,1,16,512]{3,2,1,0:T(8,128)(2,1)S(1)}, u32[]{:S(2)}, u32[]{:S(2)}) collective-permute-start(bf16[1,1,16,512]{3,2,1,0:T(8,128)(2,1)S(1)} %get-tuple-element.10), channel_id=1, source_target_pairs={{0,7},{1,8},{2,9},{3,10},{4,11},{5,12},{6,13},{7,14},{8,15},{9,0},... | collective-permute-start | bytes 49160 | tf_op jit(solution)/shard_map/ppermute | solution.py:30
  58.0 4.6 %collective-permute-start.7 = (bf16[1,1,16,512]{3,2,1,0:T(8,128)(2,1)S(1)}, bf16[1,1,16,512]{3,2,1,0:T(8,128)(2,1)S(1)}, u32[]{:S(2)}, u32[]{:S(2)}) collective-permute-start(bf16[1,1,16,512]{3,2,1,0:T(8,128)(2,1)S(1)} %get-tuple-element.9), channel_id=1, source_target_pairs={{0,8},{1,9},{2,10},{3,11},{4,12},{5,13},{6,14},{7,15},{8,0},{9,1},... | collective-permute-start | bytes 49160 | tf_op jit(solution)/shard_map/ppermute | solution.py:30
  62.6 4.1 %collective-permute-start.8 = (bf16[1,1,16,512]{3,2,1,0:T(8,128)(2,1)S(1)}, bf16[1,1,16,512]{3,2,1,0:T(8,128)(2,1)S(1)}, u32[]{:S(2)}, u32[]{:S(2)}) collective-permute-start(bf16[1,1,16,512]{3,2,1,0:T(8,128)(2,1)S(1)} %get-tuple-element.8), channel_id=1, source_target_pairs={{0,9},{1,10},{2,11},{3,12},{4,13},{5,14},{6,15},{7,0},{8,1},{9,2},... | collective-permute-start | bytes 49160 | tf_op jit(solution)/shard_map/ppermute | solution.py:30
  66.7 4.6 %collective-permute-start.9 = (bf16[1,1,16,512]{3,2,1,0:T(8,128)(2,1)S(1)}, bf16[1,1,16,512]{3,2,1,0:T(8,128)(2,1)S(1)}, u32[]{:S(2)}, u32[]{:S(2)}) collective-permute-start(bf16[1,1,16,512]{3,2,1,0:T(8,128)(2,1)S(1)} %get-tuple-element.7), channel_id=1, source_target_pairs={{0,10},{1,11},{2,12},{3,13},{4,14},{5,15},{6,0},{7,1},{8,2},{9,3},... | collective-permute-start | bytes 49160 | tf_op jit(solution)/shard_map/ppermute | solution.py:30
  71.3 3.5 %collective-permute-start.10 = (bf16[1,1,16,512]{3,2,1,0:T(8,128)(2,1)S(1)}, bf16[1,1,16,512]{3,2,1,0:T(8,128)(2,1)S(1)}, u32[]{:S(2)}, u32[]{:S(2)}) collective-permute-start(bf16[1,1,16,512]{3,2,1,0:T(8,128)(2,1)S(1)} %get-tuple-element.6), channel_id=1, source_target_pairs={{0,11},{1,12},{2,13},{3,14},{4,15},{5,0},{6,1},{7,2},{8,3},{9,4},{... | collective-permute-start | bytes 49160 | tf_op jit(solution)/shard_map/ppermute | solution.py:30
  78.0 7.2 %copy-start.1 = (bf16[256,512]{1,0:T(8,128)(2,1)}, bf16[256,512]{1,0:T(8,128)(2,1)S(1)}, u32[]{:S(2)}) copy-start(bf16[256,512]{1,0:T(8,128)(2,1)S(1)} %multiply_convert_fusion) | copy-start | bytes 786436
  83.2 2.0 %copy-start.8 = (s32[1,512]{1,0:T(1,128)S(1)}, s32[1,512]{1,0:T(1,128)}, u32[]{:S(2)}) copy-start(s32[1,512]{1,0:T(1,128)} %param.18) | copy-start | bytes 6148
  86.4 78.2 %reduce-scatter.5.cloned.1.call-start = ((), (), s32[]{:S(2)}) async-start(), calls=%async_computation.4 | async-start | bytes 2228224 | tf_op jit(solution)/shard_map/reduce_scatter | solution.py:120
  102.4 85.0 %all-reduce.2.cloned.1.call-start = ((), (), s32[]{:S(2)}) async-start(), calls=%async_computation.5 | async-start | bytes 131072 | tf_op jit(solution)/shard_map/psum | solution.py:123
Sparse Core Ops, SparseCore 0:
  86.6 12.4 reduce-scatter.2
  102.8 61.7 reduce-scatter.4
  167.4 19.8 all-reduce.1
